TPU v7x, 512 devices: a whole 4x4x16 slice. The times are simulated.
512 devices in a mesh: pages: 128 (over x, z, core), queries: 4 (over y).
Axes of the slice: x: 4, y: 4, z: 16, core: 2. Of those that a mesh axis runs over, the one named last changes fastest.
Arguments:
- query_tokens: bfloat16 [128, 32, 128], P('pages'), may hold values from -1 to 1
- page_patches: bfloat16 [256, 1536, 128], P('pages', 'queries'), may hold values from -1 to 1, as said below
- patch_counts: int32 [256], P('pages'), may hold values from 512 to 1536, as said below
- positive_page: int32 [128], replicated, may hold values from 0 to 255
Outputs:
- query_loss: float32 [128], replicated
- query_grad: float32 [128, 32, 128], P('pages', 'queries')
- page_grad: float32 [256, 1536, 128], P('pages', 'queries')
Inputs may be any that keep to these rules, and one draw needn't show every extreme that they name: `patch_counts`: each page's number of valid patches; some page has exactly 1536. `page_patches`: slots at or past a page's count hold arbitrary values.
All inputs are finite; a program needn't handle non-finite values.
Results may differ from a plain program's by a relative error of at most 0.0028.
Values may be sent and summed in bfloat16 or wider, within the bound.
A program may use at most 64 MiB of HBM per device.

v0:
```python
import jax
import jax.numpy as jnp
from jax import lax
from jax.sharding import PartitionSpec as P

smooth_tau = 0.05
page_temp = 0.02
neg_large = -1e30


def combined_all(part, axis, combine):
    gathered = jax.tree.map(lambda a: lax.all_gather(a, axis), part)

    def take(source):
        return jax.tree.map(lambda a: lax.dynamic_index_in_dim(a, source, 0, False), gathered)

    return lax.fori_loop(
        1, lax.axis_size(axis), lambda source, state: combine(state, take(source)), take(0)
    )


def merge_patch(first, second):
    highest = jnp.maximum(first[0], second[0])
    run_total = first[1] * jnp.exp((first[0] - highest) / smooth_tau) + second[1] * jnp.exp(
        (second[0] - highest) / smooth_tau
    )
    return (highest, run_total)


def merge_page(first, second):
    highest = jnp.maximum(first[0], second[0])
    run_total = first[1] * jnp.exp(first[0] - highest) + second[1] * jnp.exp(second[0] - highest)
    return (highest, run_total, first[2] + second[2])


def shards(query_tokens, page_patches, patch_counts, positive_page):
    group_slot = lax.axis_index("queries")
    gathered = lax.all_gather(query_tokens, "pages", axis=0, tiled=True)
    query_count, query_len, embed_width = gathered.shape
    token_rows = gathered.reshape(query_count * query_len, embed_width)
    row_total = token_rows.shape[0]
    block_rows = min(2048, row_total)
    block_count = row_total // block_rows
    page_local, patch_local, _ = page_patches.shape
    tile_rows = min(128, patch_local)
    live_rows = jnp.clip(patch_counts - group_slot * patch_local, 0, patch_local)
    tile_count = (live_rows + tile_rows - 1) // tile_rows
    tile_pos = jnp.arange(tile_rows, dtype=jnp.int32)

    def tile_scores(block_tokens, page_slab, live_count, tile_idx):
        row_start = tile_idx * tile_rows
        patch_tile = lax.dynamic_slice_in_dim(page_slab, row_start, tile_rows, 0)
        valid_mask = row_start + tile_pos < live_count
        similar = jnp.einsum(
            "re,pe->rp", block_tokens, patch_tile, preferred_element_type=jnp.float32
        )
        return (patch_tile, valid_mask, jnp.where(valid_mask[None, :], similar, neg_large))

    highest_list = []
    total_list = []
    score_list = []
    for page_idx in range(page_local):
        page_slab = page_patches[page_idx]
        live_count = live_rows[page_idx]
        steps_here = tile_count[page_idx]

        def forward_block(block_idx, loop_state):
            highest, run_total, score_page = loop_state
            offset = block_idx * block_rows
            block_tokens = lax.dynamic_slice_in_dim(token_rows, offset, block_rows, 0)

            def forward_tile(tile_idx, inner_state):
                run_max, run_sum, score_buf = inner_state
                _, valid_mask, masked = tile_scores(block_tokens, page_slab, live_count, tile_idx)
                new_max = jnp.maximum(run_max, jnp.max(masked, axis=1))
                fresh_terms = jnp.where(
                    valid_mask[None, :], jnp.exp((masked - new_max[:, None]) / smooth_tau), 0.0
                )
                new_sum = run_sum * jnp.exp((run_max - new_max) / smooth_tau) + jnp.sum(
                    fresh_terms, axis=1
                )
                return (new_max, new_sum, score_buf)

            start_state = (
                jnp.full((block_rows,), neg_large, jnp.float32),
                jnp.zeros((block_rows,), jnp.float32),
                score_page,
            )
            run_max, run_sum, score_page = lax.fori_loop(0, steps_here, forward_tile, start_state)
            highest = lax.dynamic_update_slice_in_dim(highest, run_max, offset, 0)
            run_total = lax.dynamic_update_slice_in_dim(run_total, run_sum, offset, 0)
            return (highest, run_total, score_page)

        score_start = jnp.zeros((1, 1), jnp.float32)
        start_page = (
            jnp.full((row_total,), neg_large, jnp.float32),
            jnp.zeros((row_total,), jnp.float32),
            score_start,
        )
        highest, run_total, score_page = lax.fori_loop(0, block_count, forward_block, start_page)
        highest_list.append(highest)
        total_list.append(run_total)
        score_list.append(score_page)
    highest, run_total = combined_all(
        (jnp.stack(highest_list), jnp.stack(total_list)), "queries", merge_patch
    )
    patch_lse = highest + smooth_tau * jnp.log(run_total)
    smooth = patch_lse - smooth_tau * jnp.log(patch_counts.astype(jnp.float32))[:, None]
    logits = smooth.reshape(page_local, query_count, query_len).sum(axis=2) / page_temp
    page_ids = lax.axis_index("pages") * page_local + jnp.arange(page_local, dtype=jnp.int32)
    is_positive = page_ids[:, None] == positive_page[None, :]
    local_max = jnp.max(logits, axis=0)
    local_sum = jnp.sum(jnp.exp(logits - local_max[None, :]), axis=0)
    local_pos = jnp.sum(jnp.where(is_positive, logits, 0.0), axis=0)
    page_max, page_sum, page_pos = combined_all(
        (local_max, local_sum, local_pos), "pages", merge_page
    )
    query_loss = page_max + jnp.log(page_sum) - page_pos
    weights = (
        jnp.exp(logits - page_max[None, :]) / page_sum[None, :] - is_positive.astype(jnp.float32)
    ) / page_temp
    row_weights = jnp.broadcast_to(
        weights[:, :, None], (page_local, query_count, query_len)
    ).reshape(page_local, row_total)
    grad_rows = jnp.zeros((row_total, embed_width), jnp.float32)
    grad_list = []
    for page_idx in range(page_local):
        page_slab = page_patches[page_idx]
        live_count = live_rows[page_idx]
        steps_here = tile_count[page_idx]
        page_lse = patch_lse[page_idx]
        page_weight = row_weights[page_idx]
        score_page = score_list[page_idx]

        def backward_block(block_idx, loop_state):
            grad_all, grad_slab = loop_state
            offset = block_idx * block_rows
            block_tokens = lax.dynamic_slice_in_dim(token_rows, offset, block_rows, 0)
            block_lse = lax.dynamic_slice_in_dim(page_lse, offset, block_rows, 0)
            block_weight = lax.dynamic_slice_in_dim(page_weight, offset, block_rows, 0)

            def backward_tile(tile_idx, inner_state):
                grad_block, slab_grad = inner_state
                row_start = tile_idx * tile_rows
                patch_tile, valid_mask, masked = tile_scores(
                    block_tokens, page_slab, live_count, tile_idx
                )
                prob_tile = jnp.where(
                    valid_mask[None, :], jnp.exp((masked - block_lse[:, None]) / smooth_tau), 0.0
                )
                coef_tile = (block_weight[:, None] * prob_tile).astype(jnp.bfloat16)
                grad_block = grad_block + jnp.dot(
                    coef_tile, patch_tile, preferred_element_type=jnp.float32
                )
                tile_grad = jnp.einsum(
                    "rp,re->pe", coef_tile, block_tokens, preferred_element_type=jnp.float32
                )
                current = lax.dynamic_slice_in_dim(slab_grad, row_start, tile_rows, 0)
                slab_grad = lax.dynamic_update_slice_in_dim(
                    slab_grad, current + tile_grad, row_start, 0
                )
                return (grad_block, slab_grad)

            grad_block = lax.dynamic_slice_in_dim(grad_all, offset, block_rows, 0)
            grad_block, grad_slab = lax.fori_loop(
                0, steps_here, backward_tile, (grad_block, grad_slab)
            )
            grad_all = lax.dynamic_update_slice_in_dim(grad_all, grad_block, offset, 0)
            return (grad_all, grad_slab)

        start_slab = jnp.zeros((patch_local, embed_width), jnp.float32)
        grad_rows, grad_slab = lax.fori_loop(
            0, block_count, backward_block, (grad_rows, start_slab)
        )
        grad_list.append(grad_slab)
    grad_work = jnp.stack(grad_list)
    grad_three = grad_rows.reshape(query_count, query_len, embed_width)
    partial_value = lax.psum_scatter(grad_three, "pages", scatter_dimension=0, tiled=True)
    query_grad = lax.psum_scatter(partial_value, "queries", scatter_dimension=1, tiled=True)
    return (query_loss, query_grad, grad_work)


def solution(mesh):
    in_specs = (P("pages", None, None), P("pages", "queries", None), P("pages"), P())
    out_specs = (P(), P("pages", "queries", None), P("pages", "queries", None))
    return jax.shard_map(shards, mesh=mesh, in_specs=in_specs, out_specs=out_specs, check_vma=False)
```

profile of v0, /device:TPU:6, one launch (start us, length us, event | category | flops | bytes accessed | tf_op | source)
XLA Modules:
  0.0 752.7 jit_solution(8003784564789250477)
XLA Ops:
  7.2 0.7 all-gather.12.cloned.1.call-update
  8.0 0.7 and_select_fusion
  8.6 0.7 fusion.51
  9.3 0.7 log_multiply_fusion
  10.0 1.0 slice_bitcast_fusion.1
  10.9 135.5 %all-gather.12.cloned.1.call-done = bf16[128,32,128]{2,1,0:T(8,128)(2,1)} async-done(((bf16[1,32,128]{2,1,0:T(8,128)(2,1)}), bf16[128,32,128]{2,1,0:T(8,128)(2,1)}) %all-gather.12.cloned.1.call-update) | async-done | bytes 1048592 | tf_op jit(solution)/shard_map/all_gather | solution.py:38
  146.4 16.4 %while.217 = (s32[]{:T(128)}, f32[4096]{0:T(1024)S(1)}, f32[4096]{0:T(1024)S(1)}, bf16[4096,128]{1,0:T(8,128)(2,1)}, s32[]{:T(128)}, /*index=5*/s32[]{:T(128)}, ...) while((s32[]{:T(128)}, f32[4096]{0:T(1024)S(1)}, ...), condition=%wide.region_11.12_spmd.clone, body=%wide.region_6.11_spmd.clone.sunk | while | flops 68688144 | bytes 3860742 | solution.py:100
  146.4 1.1 constant_dynamic-slice_fusion.17
  147.5 6.5 while.223
  148.2 0.6 add_compare_fusion.10
  150.2 0.6 add_compare_fusion.10
  152.1 0.6 add_compare_fusion.10
  154.7 1.1 constant_dynamic-slice_fusion.17
  155.8 6.5 while.223
  156.5 0.6 add_compare_fusion.10
  158.4 0.6 add_compare_fusion.10
  160.4 0.6 add_compare_fusion.10
  162.9 15.9 %while.215 = (s32[]{:T(128)}, f32[4096]{0:T(1024)S(1)}, f32[4096]{0:T(1024)S(1)}, bf16[4096,128]{1,0:T(8,128)(2,1)}, s32[]{:T(128)}, /*index=5*/s32[]{:T(128)}, ...) while((s32[]{:T(128)}, f32[4096]{0:T(1024)S(1)}, ...), condition=%wide.region_5.6_spmd.clone, body=%wide.region_0.5_spmd.clone.sunk | while | flops 68688144 | bytes 3860742 | solution.py:100
  162.9 1.1 constant_dynamic-slice_fusion.16
  164.0 6.2 while.222
  170.9 1.1 constant_dynamic-slice_fusion.16
  172.0 6.2 while.222
  178.8 12.0 %all-gather.5 = f32[4,2,4096]{2,1,0:T(2,128)S(1)} all-gather(f32[1,2,4096]{2,1,0:T(2,128)S(1)} %maximum_bitcast_fusion), channel_id=2, replica_groups=mesh['pages'=128,'queries'=4] {'queries'}, dimensions={0}, use_global_device_ids=true | all-gather | bytes 163840 | tf_op jit(solution)/shard_map/all_gather | solution.py:12
  190.8 12.0 %all-gather.6 = f32[4,2,4096]{2,1,0:T(2,128)S(1)} all-gather(f32[1,2,4096]{2,1,0:T(2,128)S(1)} %maximum_bitcast_fusion.1), channel_id=3, replica_groups=mesh['pages'=128,'queries'=4] {'queries'}, dimensions={0}, use_global_device_ids=true | all-gather | bytes 163840 | tf_op jit(solution)/shard_map/all_gather | solution.py:12
  203.6 72.6 %all-gather.7 = f32[128,1,128]{2,1,0:T(1,128)S(1)} all-gather(f32[1,1,128]{2,1,0:T(1,128)S(1)} %bitcast.124), channel_id=4, replica_groups=mesh['pages'=128,'queries'=4] {'pages'}, dimensions={0}, use_global_device_ids=true | all-gather | bytes 66048 | tf_op jit(solution)/shard_map/all_gather | solution.py:12
  276.1 72.1 %all-gather.8 = f32[128,1,128]{2,1,0:T(1,128)S(1)} all-gather(f32[1,1,128]{2,1,0:T(1,128)S(1)} %bitcast.127), channel_id=5, replica_groups=mesh['pages'=128,'queries'=4] {'pages'}, dimensions={0}, use_global_device_ids=true | all-gather | bytes 66048 | tf_op jit(solution)/shard_map/all_gather | solution.py:12
  348.2 73.1 %all-gather.9 = f32[128,1,128]{2,1,0:T(1,128)S(1)} all-gather(f32[1,1,128]{2,1,0:T(1,128)S(1)} %bitcast.126), channel_id=6, replica_groups=mesh['pages'=128,'queries'=4] {'pages'}, dimensions={0}, use_global_device_ids=true | all-gather | bytes 66048 | tf_op jit(solution)/shard_map/all_gather | solution.py:12
  421.3 6.1 while.213
  427.6 1.5 broadcast_in_dim.108
  429.1 20.6 %while.219 = (s32[]{:T(128)}, f32[4096,128]{1,0:T(8,128)}, f32[384,128]{1,0:T(8,128)S(1)}, bf16[4096,128]{1,0:T(8,128)(2,1)S(1)}, f32[4096]{0:T(1024)S(1)}, /*in...) while((s32[]{:T(128)}, f32[4096,128]{1,0:T(8,128)}, ...), condition=%wide.region_23.24_spmd.clone, body=%wide.region_20.23_spmd.clone.sunk | while | flops 203178240 | bytes 10209454 | solution.py:172
  429.2 1.3 constant_dynamic-slice_fusion.18
  430.6 7.8 %while.224 = (s32[]{:T(128)}, f32[2048,128]{1,0:T(8,128)S(1)}, f32[384,128]{1,0:T(8,128)S(1)}, s32[]{:T(128)}, f32[2048]{0:T(1024)S(1)}, /*index=5*/s32[128]{0:T...) while((s32[]{:T(128)}, f32[2048,128]{1,0:T(8,128)S(1)}, ...), condition=%wide.region_22.22_spmd, body=%wide.region_21.21_spmd.sunk | while | flops 203178240 | bytes 4932943 | solution.py:165
  438.4 1.1 constant_dynamic-update-slice_fusion.4
  439.4 1.3 constant_dynamic-slice_fusion.18
  440.8 7.8 %while.224 = (s32[]{:T(128)}, f32[2048,128]{1,0:T(8,128)S(1)}, f32[384,128]{1,0:T(8,128)S(1)}, s32[]{:T(128)}, f32[2048]{0:T(1024)S(1)}, /*index=5*/s32[128]{0:T...) while((s32[]{:T(128)}, f32[2048,128]{1,0:T(8,128)S(1)}, ...), condition=%wide.region_22.22_spmd, body=%wide.region_21.21_spmd.sunk | while | flops 203178240 | bytes 4932943 | solution.py:165
  448.6 1.1 constant_dynamic-update-slice_fusion.4
  449.9 21.1 %while.221 = (s32[]{:T(128)}, f32[4096,128]{1,0:T(8,128)}, f32[384,128]{1,0:T(8,128)S(1)}, bf16[4096,128]{1,0:T(8,128)(2,1)S(1)}, f32[4096]{0:T(1024)S(1)}, /*in...) while((s32[]{:T(128)}, f32[4096,128]{1,0:T(8,128)}, ...), condition=%wide.region_27.28_spmd.clone, body=%wide.region_24.27_spmd.clone.sunk | while | flops 203178240 | bytes 10209454 | solution.py:172
  449.9 1.3 constant_dynamic-slice_fusion.20
  451.3 8.1 %while.225 = (s32[]{:T(128)}, f32[2048,128]{1,0:T(8,128)S(1)}, f32[384,128]{1,0:T(8,128)S(1)}, s32[]{:T(128)}, f32[2048]{0:T(1024)S(1)}, /*index=5*/s32[128]{0:T...) while((s32[]{:T(128)}, f32[2048,128]{1,0:T(8,128)S(1)}, ...), condition=%wide.region_26.26_spmd, body=%wide.region_25.25_spmd.sunk | while | flops 203178240 | bytes 4932943 | solution.py:165
  452.0 0.6 add_compare_fusion.8
  459.4 1.1 constant_dynamic-update-slice_fusion.5
  460.5 1.3 constant_dynamic-slice_fusion.20
  461.9 8.1 %while.225 = (s32[]{:T(128)}, f32[2048,128]{1,0:T(8,128)S(1)}, f32[384,128]{1,0:T(8,128)S(1)}, s32[]{:T(128)}, f32[2048]{0:T(1024)S(1)}, /*index=5*/s32[128]{0:T...) while((s32[]{:T(128)}, f32[2048,128]{1,0:T(8,128)S(1)}, ...), condition=%wide.region_26.26_spmd, body=%wide.region_25.25_spmd.sunk | while | flops 203178240 | bytes 4932943 | solution.py:165
  469.9 1.1 constant_dynamic-update-slice_fusion.5
  471.1 1.3 dynamic-slice
  473.0 0.8 pad_maximum_fusion
  474.3 253.3 %reduce-scatter.3.cloned.1.call-done = f32[1,32,128]{2,1,0:T(8,128)} async-done(((f32[128,32,128]{2,1,0:T(8,128)}), f32[1,32,128]{2,1,0:T(8,128)}) %reduce-scatter.3.cloned.1.call-update) | async-done | bytes 16400 | tf_op jit(solution)/shard_map/reduce_scatter | solution.py:178
  727.6 17.7 %all-reduce = f32[1,32,128]{2,1,0:T(8,128)S(1)} all-reduce(f32[1,32,128]{2,1,0:T(8,128)} %reduce-scatter.3.cloned.1.call-done), channel_id=8, replica_groups=mesh['pages'=128,'queries'=4] {'queries'}, use_global_device_ids=true, to_apply=%region_29.30.clone | all-reduce | flops 4096 | bytes 32768
  (315 shorter events, 38.8 us)
Async XLA Ops:
  7.2 139.3 %all-gather.12.cloned.1.call-start = ((), (), s32[]{:S(2)}) async-start(), calls=%async_computation.1 | async-start | bytes 1056768 | tf_op jit(solution)/shard_map/all_gather | solution.py:38
  7.9 719.7 %reduce-scatter.3.cloned.1.call-start = ((), (), s32[]{:S(2)}) async-start(), calls=%async_computation.2 | async-start | bytes 2113536 | tf_op jit(solution)/shard_map/reduce_scatter | solution.py:178
  178.8 24.7 %copy-start.1 = (s32[128]{0:T(128)S(1)}, s32[128]{0:T(128)}, u32[]{:S(2)}) copy-start(s32[128]{0:T(128)} %param.27) | copy-start | bytes 1540
  202.8 226.3 %copy-start = (bf16[4096,128]{1,0:T(8,128)(2,1)S(1)}, bf16[4096,128]{1,0:T(8,128)(2,1)}, u32[]{:S(2)}) copy-start(bf16[4096,128]{1,0:T(8,128)(2,1)} %get-tuple-element.2438) | copy-start | bytes 3145732
Sparse Core Ops, SparseCore 0:
  10.9 135.4 all-gather.11
  471.2 256.3 reduce-scatter.2
where the time goes:
time: 754 us; the launch traced here: 753 us
  waiting for transfers between devices  390 us (52%)
  blocking collectives  259 us (34%)
  loops' own time  25.9 us (3%)
  other arithmetic  24.1 us (3%)
  local copies, waits for them, and re-layouts  22 us (3%)
  matrix products  16.9 us (2%)
  between operations  14.8 us (2%)
    reduce_scatter x1, waiting for transfers between devices, shards(): lax.psum_scatter(grad_three, 'pages', scatter_dimension=0, tiled=True)  253 us
    all_gather x5, blocking collectives, combined_all(): gathered = jax.tree.map(lambda a: lax.all_gather(a, axis), part)  242 us
    all_gather x1, waiting for transfers between devices, shards(): gathered = lax.all_gather(query_tokens, 'pages', axis=0, tiled=True)  135 us
    unnamed x1, blocking collectives  17.7 us
  transfers between devices with their start and end apart: 2, of which 2 were waited for; matrix products, arithmetic and copies ran while one was open for 1% of the time, Pallas kernels for 0%

commit v1 on v0

v1 whole, which is shorter than its diff:
```python
import functools

import jax
import jax.numpy as jnp
from jax import lax
from jax.experimental import pallas as pl
from jax.experimental.pallas import tpu as pltpu
from jax.sharding import PartitionSpec as P

smooth_tau = 0.05
page_temp = 0.02
neg_large = -1e30
chips_z = 16
lane_chunk = 256
MESH = pl.DeviceIdType.MESH
f32, bf16 = jnp.float32, jnp.bfloat16


def ring_offsets(count):
    near = sorted(range(count), key=lambda d: (min(d, count - d), d))
    return near


def onehot_dot(value, select):
    high = value.astype(bf16).astype(f32)
    rest = value - high
    mid = rest.astype(bf16).astype(f32)
    low = rest - mid
    row = lax.broadcasted_iota(jnp.int32, (8, value.shape[1]), 0)
    stack = jnp.where(row == 0, high, jnp.where(row == 1, mid, jnp.where(row == 2, low, 0.0)))
    out = jnp.dot(stack.astype(bf16), select, preferred_element_type=f32)
    return (out[0:1] + out[1:2]) + out[2:3]


def merge_lse(rows, scale):
    top = jnp.max(rows, axis=0, keepdims=True)
    total = jnp.sum(jnp.exp((rows - top) * scale), axis=0, keepdims=True)
    return (top + jnp.log(total) / scale)[0]


def kernel(
    sizes, tok_ref, pat_ref, cnt_ref, pos_ref, loss_ref, qg_ref, pg_ref,
    zbuf, zflat, gbuf, pbuf, bias, ptran, cbuf, ebuf, coef, mbuf, lbuf, erbuf, rbuf,
    softz, softx, lossbuf, sendbuf, ownbuf, recvbuf, zsum, zsend, zrecv, pgsend, pgrecv,
    local_sem, core_send, core_recv, z_send, z_recv, g_send, g_recv, l_send, l_recv,
    s_send, s_recv, x_send, x_recv, r_send, r_recv, q_send, q_recv,
):
    NX, NY, NZ = sizes
    lanes_q = NX * NZ
    query_len = tok_ref.shape[1]
    part = query_len // NY
    group = part * lanes_q
    slab = pat_ref.shape[1]
    inv_tau = 1.0 / smooth_tau
    chunk = min(lane_chunk, group)
    wide = 2 * lanes_q

    me = lax.axis_index("pages")
    y = lax.axis_index("queries")
    core = lax.rem(me, 2)
    chip = lax.div(me, 2)
    z = lax.rem(chip, NZ)
    x = lax.div(chip, NZ)

    def device(xx, yy, zz, cc):
        return ((xx * NZ + zz) * 2 + cc, yy)

    def along(pos, step, count):
        return lax.rem(pos + step, count)

    partner = device(x, y, z, 1 - core)
    z_steps = ring_offsets(NZ)[1:]
    y_steps = ring_offsets(NY)
    xy_steps = [(dx, dy) for dy in y_steps for dx in ring_offsets(NX) if (dx, dy) != (0, 0)]

    def remote(src, dst, ssem, rsem, target):
        return pltpu.make_async_remote_copy(
            src_ref=src, dst_ref=dst, send_sem=ssem, recv_sem=rsem,
            device_id=target, device_id_type=MESH,
        )

    barrier = pltpu.get_barrier_semaphore()

    def greet(target):
        pl.semaphore_signal(barrier, inc=1, device_id=target, device_id_type=MESH)

    for d in reversed(z_steps):
        greet(device(x, y, along(z, d, NZ), core))
    for dx, dy in xy_steps:
        greet(device(along(x, dx, NX), along(y, dy, NY), z, core))
    greet(partner)

    my_tokens = tok_ref.at[0, pl.ds(pl.multiple_of(y * part, part), part), :]
    own_pages = pl.ds(core * 2, 2)
    own_tokens = pltpu.make_async_copy(my_tokens, zbuf.at[z], local_sem.at[0])
    own_tokens.start()
    own_patches = pltpu.make_async_copy(pat_ref, pbuf.at[own_pages], local_sem.at[1])
    own_patches.start()
    for i in range(2):
        cbuf[core, pl.ds(i, 1), :] = jnp.full((1, cbuf.shape[2]), cnt_ref[i], jnp.int32).astype(f32)

    pl.semaphore_wait(barrier, len(z_steps) + len(xy_steps) + 1)

    z_copies = []
    for d in reversed(z_steps):
        copy = remote(
            my_tokens, zbuf.at[z], z_send.at[d], z_recv.at[d], device(x, y, along(z, d, NZ), core)
        )
        copy.start()
        z_copies.append(copy)
    swap_patches = remote(
        pat_ref, pbuf.at[own_pages], core_send.at[0], core_recv.at[0], partner
    )
    swap_patches.start()
    swap_counts = remote(cbuf.at[core], cbuf.at[core], core_send.at[1], core_recv.at[1], partner)
    swap_counts.start()

    own_patches.wait()
    swap_counts.wait_recv()
    swap_patches.wait_recv()
    depth = pbuf.shape[2]
    slot = y * slab + lax.broadcasted_iota(jnp.int32, (slab, depth), 0)
    first_lane = lax.broadcasted_iota(jnp.int32, (slab, depth), 1) == 0
    for p in range(4):
        count = cbuf[p // 2, pl.ds(p % 2, 1), :].astype(jnp.int32)
        dead = jnp.logical_and(slot >= count, first_lane)
        bias[p] = jnp.where(dead, neg_large, 0.0).astype(bf16)
        ptran[:, p * slab : (p + 1) * slab] = pbuf[p].astype(f32).T.astype(bf16)
    select = (
        lax.broadcasted_iota(jnp.int32, (2 * lanes_q, wide), 0)
        == 2 * lax.rem(lax.broadcasted_iota(jnp.int32, (2 * lanes_q, wide), 1), lanes_q) + core
    )
    positive = jnp.dot(
        jnp.broadcast_to(pos_ref[...].astype(f32), (8, 2 * lanes_q)).astype(bf16),
        select.astype(bf16), preferred_element_type=f32,
    )[0:1]
    log_count = smooth_tau * jnp.log(
        jnp.concatenate([cbuf[0, 0:2, 0:wide], cbuf[1, 0:2, 0:wide]], axis=0)
    )

    own_tokens.wait()
    for copy in z_copies:
        copy.wait_recv()
    zflat[...] = zbuf[...].astype(f32).reshape(zflat.shape)
    for t in range(part):
        gbuf[y * part + t, x] = zflat[pl.ds(t, NZ, stride=part), :].astype(bf16)

    g_copies = {}
    mine = gbuf.at[pl.ds(y * part, part), x]
    for n, (dx, dy) in enumerate(xy_steps):
        copy = remote(
            mine, mine, g_send.at[n], g_recv.at[n],
            device(along(x, dx, NX), along(y, dy, NY), z, core),
        )
        copy.start()
        g_copies[dx, dy] = copy

    ones = jnp.where(lax.broadcasted_iota(jnp.int32, (chunk, depth), 1) == 0, 1.0, 0.0).astype(bf16)
    rows_t = chunk // lanes_q
    l_copies = []
    for k, back in enumerate(y_steps):
        for dx in range(NX):
            if (dx, back) in g_copies:
                g_copies[dx, back].wait_recv()
        gy = along(y, NY - back, NY)

        def forward(step, carry):
            p = lax.div(step, group // chunk)
            piece = lax.rem(step, group // chunk)
            tokens = gbuf[pl.ds(gy * part + piece * rows_t, rows_t)].reshape(chunk, depth)
            similar = lax.dot_general(
                jnp.concatenate([pbuf[p], bias[p]], axis=1),
                jnp.concatenate([tokens, ones], axis=1),
                (((1,), (1,)), ((), ())), preferred_element_type=f32,
            )
            top = jnp.max(similar, axis=0, keepdims=True)
            terms = jnp.exp((similar - top) * inv_tau)
            lanes = pl.ds(pl.multiple_of(piece * chunk, chunk), chunk)
            ebuf[gy, p, :, lanes] = terms
            total = jnp.sum(terms, axis=0, keepdims=True)
            mbuf[gy, pl.ds(p, 1), lanes] = top
            lbuf[y, gy, pl.ds(p, 1), lanes] = top + smooth_tau * jnp.log(total)
            return carry

        lax.fori_loop(0, 4 * (group // chunk), forward, 0)
        for n, dy in enumerate(y_steps[1:]):
            copy = remote(
                lbuf.at[y, gy], lbuf.at[y, gy], l_send.at[k, n], l_recv.at[k, n],
                device(x, along(y, dy, NY), z, core),
            )
            copy.start()
            l_copies.append(copy)

    for copy in l_copies:
        copy.wait_recv()
    sums = jnp.zeros((4, wide), f32)
    for g in range(NY):
        lse = merge_lse(lbuf[:, g], inv_tau)
        erbuf[g] = jnp.exp((mbuf[g] - lse) * inv_tau)
        for i in range(group // wide):
            sums = sums + lse[:, i * wide : (i + 1) * wide]
    sums = sums + pltpu.roll(sums, lanes_q, 1)
    logits = (sums - query_len * log_count) / page_temp
    page_id = (chip * 4 + lax.broadcasted_iota(jnp.int32, (4, wide), 0)).astype(f32)
    is_positive = page_id == positive

    softz[z, 0:1, :] = merge_lse(logits[:, None, :], 1.0)
    softz[z, 1:2, :] = jnp.sum(jnp.where(is_positive, logits, 0.0), axis=0, keepdims=True)
    s_copies = []
    for d in reversed(z_steps):
        copy = remote(
            softz.at[z], softz.at[z], s_send.at[d], s_recv.at[d],
            device(x, y, along(z, d, NZ), core),
        )
        copy.start()
        s_copies.append(copy)
    for copy in s_copies:
        copy.wait_recv()
    softx[x, 0:1, :] = merge_lse(softz[:, 0:1, :], 1.0)
    softx[x, 1:2, :] = jnp.sum(softz[:, 1:2, :], axis=0)
    x_copies = []
    for d in ring_offsets(NX)[1:]:
        copy = remote(
            softx.at[x], softx.at[x], x_send.at[d], x_recv.at[d],
            device(along(x, d, NX), y, z, core),
        )
        copy.start()
        x_copies.append(copy)
    for copy in x_copies:
        copy.wait_recv()
    all_lse = merge_lse(softx[:, 0:1, :], 1.0)
    lossbuf[core] = all_lse - jnp.sum(softx[:, 1:2, :], axis=0)
    swap_loss = remote(lossbuf.at[core], lossbuf.at[core], core_send.at[2], core_recv.at[2], partner)
    swap_loss.start()
    weights = (jnp.exp(logits - all_lse) - is_positive.astype(f32)) / page_temp
    wide_weights = jnp.concatenate([weights] * (group // wide), axis=1)
    for g in range(NY):
        rbuf[g] = erbuf[g] * wide_weights

    r_copies = []
    for back in reversed(y_steps):
        gy = along(y, NY - back, NY)

        def backward(p, carry):
            coef[gy, p] = (ebuf[gy, p] * rbuf[gy, pl.ds(p, 1), :]).astype(bf16)
            return carry

        lax.fori_loop(0, 4, backward, 0)

        def grads(piece, carry):
            lanes = pl.ds(pl.multiple_of(piece * chunk, chunk), chunk)
            across = jnp.dot(
                ptran[...], coef[gy, :, :, lanes].reshape(4 * slab, chunk),
                preferred_element_type=f32,
            )
            rows = across.T.reshape(rows_t, NX, NZ, depth)
            sendbuf[pl.ds(gy * part + piece * rows_t, rows_t)] = rows.astype(bf16)
            if back == 0:
                ownbuf[pl.ds(piece * rows_t, rows_t)] = rows
            return carry

        lax.fori_loop(0, group // chunk, grads, 0)
        for dx in range(NX):
            dy = (NY - back) % NY
            if (dx, dy) == (0, 0):
                continue
            n = xy_steps.index((dx, dy))
            xx = along(x, dx, NX)
            copy = remote(
                sendbuf.at[pl.ds(gy * part, part), xx], recvbuf.at[x * NY + y],
                r_send.at[n], r_recv.at[n], device(xx, gy, z, core),
            )
            copy.start()
            r_copies.append((copy, dx, dy))

    def page_part(p):
        total = jnp.zeros((slab, depth), f32)
        for g in range(NY):
            tokens = gbuf[g * part : (g + 1) * part].reshape(group, depth)
            total = total + jnp.dot(coef[g, p], tokens, preferred_element_type=f32)
        return total

    def other_pages(i, carry):
        pgsend[i] = page_part(2 * (1 - core) + i)
        return carry

    lax.fori_loop(0, 2, other_pages, 0)
    swap_grads = remote(pgsend, pgrecv, core_send.at[3], core_recv.at[3], partner)
    swap_grads.start()

    total = ownbuf[:, pl.ds(x, 1)].reshape(part * NZ, depth)
    for copy, dx, dy in r_copies:
        copy.wait_recv()
        source = along(x, NX - dx, NX) * NY + along(y, NY - dy, NY)
        total = total + recvbuf[source].astype(f32).reshape(part * NZ, depth)
    zsum[...] = total
    for zz in range(NZ):
        zsend[zz] = zsum[pl.ds(zz, part, stride=NZ), :]
    q_copies = []
    for d in reversed(z_steps):
        zz = along(z, d, NZ)
        copy = remote(
            zsend.at[zz], zrecv.at[z], q_send.at[d], q_recv.at[d], device(x, y, zz, core)
        )
        copy.start()
        q_copies.append((copy, d))

    def own_page(i, carry):
        pg_ref[i] = page_part(2 * core + i)
        return carry

    lax.fori_loop(0, 2, own_page, 0)
    swap_grads.wait_recv()
    pg_ref[...] += pgrecv[...]

    swap_loss.wait_recv()
    row = lax.broadcasted_iota(jnp.int32, (wide, 2 * lanes_q), 0)
    col = lax.broadcasted_iota(jnp.int32, (wide, 2 * lanes_q), 1)
    loss = jnp.zeros((1, 2 * lanes_q), f32)
    for c in range(2):
        spread = jnp.logical_and(col == 2 * row + c, row < lanes_q).astype(f32).astype(bf16)
        loss = loss + onehot_dot(lossbuf[c], spread)
    loss_ref[...] = loss

    total = zsend[z]
    for copy, d in q_copies:
        copy.wait_recv()
        total = total + zrecv[along(z, NZ - d, NZ)]
    qg_ref[0] = total

    for copy in z_copies + list(g_copies.values()) + l_copies + s_copies + x_copies:
        copy.wait_send()
    for copy in [swap_patches, swap_counts, swap_loss, swap_grads]:
        copy.wait_send()
    for copy, *_ in r_copies + q_copies:
        copy.wait_send()


def shards(sizes, query_tokens, page_patches, patch_counts, positive_page):
    NX, NY, NZ = sizes
    _, query_len, depth = query_tokens.shape
    slab = page_patches.shape[1]
    part = query_len // NY
    lanes_q = NX * NZ
    group = part * lanes_q
    wide = 2 * lanes_q
    peers = NX * NY - 1
    vmem = pltpu.VMEM
    dma = pltpu.SemaphoreType.DMA
    loss, query_grad, page_grad = pl.pallas_call(
        functools.partial(kernel, sizes),
        out_shape=(
            jax.ShapeDtypeStruct((1, 2 * lanes_q), f32),
            jax.ShapeDtypeStruct((1, part, depth), f32),
            jax.ShapeDtypeStruct((2, slab, depth), f32),
        ),
        in_specs=[
            pl.BlockSpec(memory_space=pltpu.VMEM),
            pl.BlockSpec(memory_space=pltpu.VMEM),
            pl.BlockSpec(memory_space=pltpu.SMEM),
            pl.BlockSpec(memory_space=pltpu.VMEM),
        ],
        out_specs=[pl.BlockSpec(memory_space=pltpu.VMEM)] * 3,
        scratch_shapes=[
            vmem((NZ, part, depth), bf16),
            vmem((NZ * part, depth), f32),
            vmem((query_len, NX, NZ, depth), bf16),
            vmem((4, slab, depth), bf16),
            vmem((4, slab, depth), bf16),
            vmem((depth, 4 * slab), bf16),
            vmem((2, 8, depth), f32),
            vmem((NY, 4, slab, group), f32),
            vmem((NY, 4, slab, group), bf16),
            vmem((NY, 4, group), f32),
            vmem((NY, NY, 4, group), f32),
            vmem((NY, 4, group), f32),
            vmem((NY, 4, group), f32),
            vmem((NZ, 2, wide), f32),
            vmem((NX, 2, wide), f32),
            vmem((2, 1, wide), f32),
            vmem((query_len, NX, NZ, depth), bf16),
            vmem((part, NX, NZ, depth), f32),
            vmem((NX * NY, part, NZ, depth), bf16),
            vmem((part * NZ, depth), f32),
            vmem((NZ, part, depth), f32),
            vmem((NZ, part, depth), f32),
            vmem((2, slab, depth), f32),
            vmem((2, slab, depth), f32),
            dma((2,)),
            dma((4,)), dma((4,)),
            dma((NZ,)), dma((NZ,)),
            dma((peers,)), dma((peers,)),
            dma((NY, NY - 1)), dma((NY, NY - 1)),
            dma((NZ,)), dma((NZ,)),
            dma((NX,)), dma((NX,)),
            dma((peers,)), dma((peers,)),
            dma((NZ,)), dma((NZ,)),
        ],
        compiler_params=pltpu.CompilerParams(
            collective_id=0, has_side_effects=True, vmem_limit_bytes=56 * 1024 * 1024
        ),
    )(query_tokens, page_patches, patch_counts, positive_page.reshape(1, 2 * lanes_q))
    return (loss.reshape(2 * lanes_q), query_grad, page_grad)


def solution(mesh):
    chips = mesh.shape["pages"] // 2
    sizes = (chips // chips_z, mesh.shape["queries"], chips_z)
    in_specs = (P("pages", None, None), P("pages", "queries", None), P("pages"), P())
    out_specs = (P(), P("pages", "queries", None), P("pages", "queries", None))
    return jax.shard_map(
        functools.partial(shards, sizes),
        mesh=mesh, in_specs=in_specs, out_specs=out_specs, check_vma=False,
    )
```

time: 754 us -> 75.6 us (0.10)
  waiting for transfers between devices: 390 us -> 0 us
  blocking collectives: 259 us -> 0 us
  Pallas kernels: 0 us -> 70.1 us
  loops' own time: 25.9 us -> 0 us
  other arithmetic: 24.1 us -> 0 us
  local copies, waits for them, and re-layouts: 22 us -> 3.53 us
  matrix products: 16.9 us -> 0 us
  between operations: 14.8 us -> 0.66 us
    reduce_scatter x1 -> x0, waiting for transfers between devices: 253 us -> none  [shards(): lax.psum_scatter(grad_three, 'pages', scatter_dimension=0, tiled=True)]
    all_gather x5 -> x0, blocking collectives: 242 us -> none  [combined_all(): gathered = jax.tree.map(lambda a: lax.all_gather(a, axis), part)]
    all_gather x1 -> x0, waiting for transfers between devices: 135 us -> none  [shards(): gathered = lax.all_gather(query_tokens, 'pages', axis=0, tiled=True)]
    pallas_call x0 -> x1, Pallas kernels: none -> 70.1 us  [shards(): pl.pallas_call(functools.partial(kernel, sizes), out_shape=(jax.ShapeDtyp...]
    another operation x14 -> x0, loops' own time: 25.9 us -> none  [the longest x4 11.5 us: forward_block(): lax.fori_loop(0, steps_here, forward_tile, start_state)]
    unnamed x1 -> x0, blocking collectives: 17.7 us -> none
    dot_general x48 -> x0, matrix products: 16.9 us -> none  [the longest x24 8.95 us: tile_scores(): jnp.einsum('re,pe->rp', block_tokens, patch_tile, preferred_element_type=...]
    lt x24 -> x0, other arithmetic: 14.1 us -> none  [tile_scores(): valid_mask = row_start + tile_pos < live_count]
  transfers between devices with their start and end apart: 2 -> 0, of which waited for: 2 -> 0; matrix products, arithmetic and copies ran while one was open for 1% -> 0% of each run, Pallas kernels for 0% -> 0%
where the time goes in v1:
time: 75.6 us; the launch traced here: 74.3 us
  Pallas kernels  70.1 us (93%)
  local copies, waits for them, and re-layouts  3.53 us (5%)
    pallas_call x1, Pallas kernels, shards(): pl.pallas_call(functools.partial(kernel, sizes), out_shape=(jax.ShapeDtyp...  70.1 us
    unnamed x7, local copies, waits for them, and re-layouts  3.53 us

profile of v1, /device:TPU:6, one launch (start us, length us, event | category | flops | bytes accessed | tf_op | source)
XLA Modules:
  0.0 74.3 jit_solution(7532583300463475562)
XLA Ops:
  0.6 70.1 %shard_map.67 = (f32[1,128]{1,0:T(1,128)}, f32[1,8,128]{2,1,0:T(8,128)}, f32[2,384,128]{2,1,0:T(8,128)}) custom-call(bf16[1,32,128]{2,1,0:T(8,128)(2,1)} %tok_ref.1, bf16[2,384,128]{2,1,0:T(8,128)(2,1)} %pat_ref.1, s32[2]{0:T(128)} %cnt_ref.1, s32[1,128]{1,0:T(1,128)} %bitcast.2), custom_call_target="tpu_custom_call" | custom-call | tf_op jit(solution)/shard_map/pallas_call | solution.py:350
  70.8 0.0 copy-start
  70.8 0.0 copy-start.1
  70.8 0.7 copy-done.1
  71.4 0.5 copy.10
  71.9 0.0 copy-done
  71.9 0.6 copy.11
  72.5 1.8 %copy.12 = f32[2,384,128]{2,1,0:T(8,128)} copy(f32[2,384,128]{2,1,0:T(8,128)} %get-tuple-element.14) | data formatting | bytes 786432
Async XLA Ops:
  70.8 1.2 %copy-start = (f32[1,8,128]{2,1,0:T(8,128)S(1)}, f32[1,8,128]{2,1,0:T(8,128)}, u32[]{:S(2)}) copy-start(f32[1,8,128]{2,1,0:T(8,128)} %get-tuple-element.13) | copy-start | bytes 12292
  70.8 0.7 copy-start.1

commit v2 on v1

--- a/solution.py
+++ b/solution.py
@@ -1,4 +1,5 @@
 import functools
+import math
 
 import jax
 import jax.numpy as jnp
@@ -40,8 +41,9 @@
 
 def kernel(
     sizes, tok_ref, pat_ref, cnt_ref, pos_ref, loss_ref, qg_ref, pg_ref,
+    counts, pos_row, loss_row, qg_tile, pg_tile,
     zbuf, zflat, gbuf, pbuf, bias, ptran, cbuf, ebuf, coef, mbuf, lbuf, erbuf, rbuf,
-    softz, softx, lossbuf, sendbuf, ownbuf, recvbuf, zsum, zsend, zrecv, pgsend, pgrecv,
+    held_a, held_b, softz, softx, lossbuf, sendbuf, ownbuf, recvbuf, zsum, zsend, zrecv, pgsend, pgrecv,
     local_sem, core_send, core_recv, z_send, z_recv, g_send, g_recv, l_send, l_recv,
     s_send, s_recv, x_send, x_recv, r_send, r_recv, q_send, q_recv,
 ):
@@ -51,7 +53,9 @@
     part = query_len // NY
     group = part * lanes_q
     slab = pat_ref.shape[1]
+    held = (held_a, held_b)
     inv_tau = 1.0 / smooth_tau
+    exp_scale = inv_tau * math.log2(math.e)
     chunk = min(lane_chunk, group)
     wide = 2 * lanes_q
 
@@ -92,12 +96,17 @@
 
     my_tokens = tok_ref.at[0, pl.ds(pl.multiple_of(y * part, part), part), :]
     own_pages = pl.ds(core * 2, 2)
+    own_counts = pltpu.make_async_copy(cnt_ref, counts, local_sem.at[2])
+    own_counts.start()
+    own_pos = pltpu.make_async_copy(pos_ref, pos_row, local_sem.at[3])
+    own_pos.start()
     own_tokens = pltpu.make_async_copy(my_tokens, zbuf.at[z], local_sem.at[0])
     own_tokens.start()
     own_patches = pltpu.make_async_copy(pat_ref, pbuf.at[own_pages], local_sem.at[1])
     own_patches.start()
+    own_counts.wait()
     for i in range(2):
-        cbuf[core, pl.ds(i, 1), :] = jnp.full((1, cbuf.shape[2]), cnt_ref[i], jnp.int32).astype(f32)
+        cbuf[core, pl.ds(i, 1), :] = jnp.full((1, cbuf.shape[2]), counts[i], jnp.int32).astype(f32)
 
     pl.semaphore_wait(barrier, len(z_steps) + len(xy_steps) + 1)
 
@@ -130,8 +139,9 @@
         lax.broadcasted_iota(jnp.int32, (2 * lanes_q, wide), 0)
         == 2 * lax.rem(lax.broadcasted_iota(jnp.int32, (2 * lanes_q, wide), 1), lanes_q) + core
     )
+    own_pos.wait()
     positive = jnp.dot(
-        jnp.broadcast_to(pos_ref[...].astype(f32), (8, 2 * lanes_q)).astype(bf16),
+        jnp.broadcast_to(pos_row[...].astype(f32), (8, 2 * lanes_q)).astype(bf16),
         select.astype(bf16), preferred_element_type=f32,
     )[0:1]
     log_count = smooth_tau * jnp.log(
@@ -164,25 +174,32 @@
                 g_copies[dx, back].wait_recv()
         gy = along(y, NY - back, NY)
 
-        def forward(step, carry):
-            p = lax.div(step, group // chunk)
-            piece = lax.rem(step, group // chunk)
+        def scores(block):
+            p, piece = block % 4, block // 4
             tokens = gbuf[pl.ds(gy * part + piece * rows_t, rows_t)].reshape(chunk, depth)
             similar = lax.dot_general(
                 jnp.concatenate([pbuf[p], bias[p]], axis=1),
                 jnp.concatenate([tokens, ones], axis=1),
                 (((1,), (1,)), ((), ())), preferred_element_type=f32,
             )
-            top = jnp.max(similar, axis=0, keepdims=True)
-            terms = jnp.exp((similar - top) * inv_tau)
-            lanes = pl.ds(pl.multiple_of(piece * chunk, chunk), chunk)
+            held[block % 2][...] = similar
+            return jnp.max(similar, axis=0, keepdims=True)
+
+        def exponents(block, top):
+            p, piece = block % 4, block // 4
+            lanes = slice(piece * chunk, (piece + 1) * chunk)
+            terms = jnp.exp2((held[block % 2][...] - top) * exp_scale)
             ebuf[gy, p, :, lanes] = terms
             total = jnp.sum(terms, axis=0, keepdims=True)
-            mbuf[gy, pl.ds(p, 1), lanes] = top
-            lbuf[y, gy, pl.ds(p, 1), lanes] = top + smooth_tau * jnp.log(total)
-            return carry
-
-        lax.fori_loop(0, 4 * (group // chunk), forward, 0)
+            mbuf[gy, p : p + 1, lanes] = top
+            lbuf[y, gy, p : p + 1, lanes] = top + smooth_tau * jnp.log(total)
+
+        blocks = 4 * (group // chunk)
+        top = scores(0)
+        for block in range(blocks):
+            following = scores(block + 1) if block + 1 < blocks else None
+            exponents(block, top)
+            top = following
         for n, dy in enumerate(y_steps[1:]):
             copy = remote(
                 lbuf.at[y, gy], lbuf.at[y, gy], l_send.at[k, n], l_recv.at[k, n],
@@ -306,12 +323,14 @@
         q_copies.append((copy, d))
 
     def own_page(i, carry):
-        pg_ref[i] = page_part(2 * core + i)
+        pg_tile[i] = page_part(2 * core + i)
         return carry
 
     lax.fori_loop(0, 2, own_page, 0)
     swap_grads.wait_recv()
-    pg_ref[...] += pgrecv[...]
+    pg_tile[...] += pgrecv[...]
+    outs = [pltpu.make_async_copy(pg_tile, pg_ref, local_sem.at[4])]
+    outs[0].start()
 
     swap_loss.wait_recv()
     row = lax.broadcasted_iota(jnp.int32, (wide, 2 * lanes_q), 0)
@@ -320,13 +339,17 @@
     for c in range(2):
         spread = jnp.logical_and(col == 2 * row + c, row < lanes_q).astype(f32).astype(bf16)
         loss = loss + onehot_dot(lossbuf[c], spread)
-    loss_ref[...] = loss
+    loss_row[...] = loss
+    outs.append(pltpu.make_async_copy(loss_row, loss_ref, local_sem.at[5]))
+    outs[1].start()
 
     total = zsend[z]
     for copy, d in q_copies:
         copy.wait_recv()
         total = total + zrecv[along(z, NZ - d, NZ)]
-    qg_ref[0] = total
+    qg_tile[0] = total
+    outs.append(pltpu.make_async_copy(qg_tile, qg_ref, local_sem.at[6]))
+    outs[2].start()
 
     for copy in z_copies + list(g_copies.values()) + l_copies + s_copies + x_copies:
         copy.wait_send()
@@ -334,6 +357,21 @@
         copy.wait_send()
     for copy, *_ in r_copies + q_copies:
         copy.wait_send()
+    for copy in outs:
+        copy.wait()
+
+
+def hand_on(*refs):
+    sources, targets, tiles, sem = refs[:3], refs[3:6], refs[6:9], refs[9]
+    takes = [pltpu.make_async_copy(s, t, sem.at[i]) for i, (s, t) in enumerate(zip(sources, tiles))]
+    gives = [pltpu.make_async_copy(t, o, sem.at[i]) for i, (t, o) in enumerate(zip(tiles, targets))]
+    for copy in takes:
+        copy.start()
+    for take, give in zip(takes, gives):
+        take.wait()
+        give.start()
+    for copy in gives:
+        copy.wait()
 
 
 def shards(sizes, query_tokens, page_patches, patch_counts, positive_page):
@@ -347,21 +385,23 @@
     peers = NX * NY - 1
     vmem = pltpu.VMEM
     dma = pltpu.SemaphoreType.DMA
+    shapes = [
+        jax.ShapeDtypeStruct((2, slab, depth), f32),
+        jax.ShapeDtypeStruct((1, part, depth), f32),
+        jax.ShapeDtypeStruct((1, 2 * lanes_q), f32),
+    ]
+    hbm = pl.BlockSpec(memory_space=pltpu.HBM)
     loss, query_grad, page_grad = pl.pallas_call(
         functools.partial(kernel, sizes),
-        out_shape=(
-            jax.ShapeDtypeStruct((1, 2 * lanes_q), f32),
-            jax.ShapeDtypeStruct((1, part, depth), f32),
-            jax.ShapeDtypeStruct((2, slab, depth), f32),
-        ),
-        in_specs=[
-            pl.BlockSpec(memory_space=pltpu.VMEM),
-            pl.BlockSpec(memory_space=pltpu.VMEM),
-            pl.BlockSpec(memory_space=pltpu.SMEM),
-            pl.BlockSpec(memory_space=pltpu.VMEM),
-        ],
-        out_specs=[pl.BlockSpec(memory_space=pltpu.VMEM)] * 3,
+        out_shape=shapes[::-1],
+        in_specs=[hbm] * 4,
+        out_specs=[hbm] * 3,
         scratch_shapes=[
+            pltpu.SMEM((2,), jnp.int32),
+            vmem((1, 2 * lanes_q), jnp.int32),
+            vmem((1, 2 * lanes_q), f32),
+            vmem((1, part, depth), f32),
+            vmem((2, slab, depth), f32),
             vmem((NZ, part, depth), bf16),
             vmem((NZ * part, depth), f32),
             vmem((query_len, NX, NZ, depth), bf16),
@@ -375,6 +415,8 @@
             vmem((NY, NY, 4, group), f32),
             vmem((NY, 4, group), f32),
             vmem((NY, 4, group), f32),
+            vmem((slab, min(lane_chunk, group)), f32),
+            vmem((slab, min(lane_chunk, group)), f32),
             vmem((NZ, 2, wide), f32),
             vmem((NX, 2, wide), f32),
             vmem((2, 1, wide), f32),
@@ -386,7 +428,7 @@
             vmem((NZ, part, depth), f32),
             vmem((2, slab, depth), f32),
             vmem((2, slab, depth), f32),
-            dma((2,)),
+            dma((7,)),
             dma((4,)), dma((4,)),
             dma((NZ,)), dma((NZ,)),
             dma((peers,)), dma((peers,)),
@@ -400,6 +442,13 @@
             collective_id=0, has_side_effects=True, vmem_limit_bytes=56 * 1024 * 1024
         ),
     )(query_tokens, page_patches, patch_counts, positive_page.reshape(1, 2 * lanes_q))
+    page_grad, query_grad, loss = pl.pallas_call(
+        hand_on,
+        out_shape=shapes,
+        in_specs=[hbm] * 3,
+        out_specs=[hbm] * 3,
+        scratch_shapes=[vmem(shape.shape, f32) for shape in shapes] + [dma((3,))],
+    )(page_grad, query_grad, loss)
     return (loss.reshape(2 * lanes_q), query_grad, page_grad)
 
 

time: 75.6 us -> 65.9 us (0.87); the launches traced: 74.3 us -> 65.4 us
  Pallas kernels: 70.1 us -> 64.8 us
  local copies, waits for them, and re-layouts: 3.53 us -> 0 us
    pallas_call x1 -> x2, Pallas kernels: 70.1 us -> 64.8 us  [the longest x1 63 us: shards(): pl.pallas_call(functools.partial(kernel, sizes), out_shape=shapes[::-1],...]
    unnamed x7 -> x0, local copies, waits for them, and re-layouts: 3.53 us -> none
where the time goes in v2:
time: 65.9 us; the launch traced here: 65.4 us
  Pallas kernels  64.8 us (98%)
    pallas_call x1, Pallas kernels, shards(): pl.pallas_call(functools.partial(kernel, sizes), out_shape=shapes[::-1],...  63 us
    pallas_call x1, Pallas kernels, shards(): pl.pallas_call(hand_on, out_shape=shapes, in_specs=[hbm] * 3, out_specs=[...  1.77 us

profile of v2, /device:TPU:6, one launch (start us, length us, event | category | flops | bytes accessed | tf_op | source)
XLA Modules:
  0.0 65.4 jit_solution(5085241057099044180)
XLA Ops:
  0.6 63.0 %shard_map.67 = (f32[1,128]{1,0:T(1,128)}, f32[1,8,128]{2,1,0:T(8,128)}, f32[2,384,128]{2,1,0:T(8,128)}) custom-call(bf16[1,32,128]{2,1,0:T(8,128)(2,1)} %tok_ref.1, bf16[2,384,128]{2,1,0:T(8,128)(2,1)} %pat_ref.1, s32[2]{0:T(128)} %cnt_ref.1, s32[1,128]{1,0:T(1,128)} %bitcast.2), custom_call_target="tpu_custom_call" | custom-call | tf_op jit(solution)/shard_map/pallas_call | solution.py:394
  63.6 1.8 %shard_map.68 = (f32[2,384,128]{2,1,0:T(8,128)}, f32[1,8,128]{2,1,0:T(8,128)}, f32[1,128]{1,0:T(1,128)}) custom-call(f32[2,384,128]{2,1,0:T(8,128)} %get-tuple-element.9.refs_0_, f32[1,8,128]{2,1,0:T(8,128)} %get-tuple-element.10.refs_1_, f32[1,128]{1,0:T(1,128)} %get-tuple-element.11.refs_2_), custom_call_target="tpu_custom_call" | custom-call | tf_op jit(solution)/shard_map/pallas_call | solution.py:445

commit v3 on v2

--- a/solution.py
+++ b/solution.py
@@ -42,9 +42,9 @@
 def kernel(
     sizes, tok_ref, pat_ref, cnt_ref, pos_ref, loss_ref, qg_ref, pg_ref,
     counts, pos_row, loss_row, qg_tile, pg_tile,
-    zbuf, zflat, gbuf, pbuf, bias, ptran, cbuf, ebuf, coef, mbuf, lbuf, erbuf, rbuf,
+    zbuf, zflat, stage, gbuf, pbuf, bias, ptran, cbuf, ebuf, coef, mbuf, lbuf, erbuf, rbuf,
     held_a, held_b, softz, softx, lossbuf, sendbuf, ownbuf, recvbuf, zsum, zsend, zrecv, pgsend, pgrecv,
-    local_sem, core_send, core_recv, z_send, z_recv, g_send, g_recv, l_send, l_recv,
+    ready, local_sem, core_send, core_recv, z_send, z_recv, g_send, g_recv, l_send, l_recv,
     s_send, s_recv, x_send, x_recv, r_send, r_recv, q_send, q_recv,
 ):
     NX, NY, NZ = sizes
@@ -88,11 +88,14 @@
     def greet(target):
         pl.semaphore_signal(barrier, inc=1, device_id=target, device_id_type=MESH)
 
-    for d in reversed(z_steps):
-        greet(device(x, y, along(z, d, NZ), core))
-    for dx, dy in xy_steps:
-        greet(device(along(x, dx, NX), along(y, dy, NY), z, core))
-    greet(partner)
+    @pl.when(core == 0)
+    def _():
+        for cc in range(2):
+            for d in reversed(z_steps):
+                greet(device(x, y, along(z, d, NZ), cc))
+            for dx, dy in xy_steps:
+                greet(device(along(x, dx, NX), along(y, dy, NY), z, cc))
+        greet(partner)
 
     my_tokens = tok_ref.at[0, pl.ds(pl.multiple_of(y * part, part), part), :]
     own_pages = pl.ds(core * 2, 2)
@@ -100,7 +103,7 @@
     own_counts.start()
     own_pos = pltpu.make_async_copy(pos_ref, pos_row, local_sem.at[3])
     own_pos.start()
-    own_tokens = pltpu.make_async_copy(my_tokens, zbuf.at[z], local_sem.at[0])
+    own_tokens = pltpu.make_async_copy(my_tokens, zbuf.at[core, z], local_sem.at[0])
     own_tokens.start()
     own_patches = pltpu.make_async_copy(pat_ref, pbuf.at[own_pages], local_sem.at[1])
     own_patches.start()
@@ -108,20 +111,38 @@
     for i in range(2):
         cbuf[core, pl.ds(i, 1), :] = jnp.full((1, cbuf.shape[2]), counts[i], jnp.int32).astype(f32)
 
-    pl.semaphore_wait(barrier, len(z_steps) + len(xy_steps) + 1)
-
-    z_copies = []
+    pl.semaphore_wait(barrier, len(z_steps) + len(xy_steps) + core)
+
+    @pl.when(core == 1)
+    def _():
+        for dx, dy in xy_steps:
+            pl.semaphore_signal(
+                ready, inc=1, device_id=device(along(x, dx, NX), along(y, dy, NY), z, 0),
+                device_id_type=MESH,
+            )
+
+    def z_copy(source_core, d):
+        return remote(
+            my_tokens, zbuf.at[source_core, z], z_send.at[d], z_recv.at[source_core, d],
+            device(x, y, along(z, d, NZ), 0),
+        )
+
     for d in reversed(z_steps):
-        copy = remote(
-            my_tokens, zbuf.at[z], z_send.at[d], z_recv.at[d], device(x, y, along(z, d, NZ), core)
-        )
-        copy.start()
-        z_copies.append(copy)
+        z_copy(core, d).start()
     swap_patches = remote(
         pat_ref, pbuf.at[own_pages], core_send.at[0], core_recv.at[0], partner
     )
+    swap_counts = remote(cbuf.at[core], cbuf.at[core], core_send.at[1], core_recv.at[1], partner)
+
+    @pl.when(core == 1)
+    def _():
+        z_copy(1, 0).start()
+
+    @pl.when(core == 0)
+    def _():
+        z_copy(1, 0).wait_recv()
+
     swap_patches.start()
-    swap_counts = remote(cbuf.at[core], cbuf.at[core], core_send.at[1], core_recv.at[1], partner)
     swap_counts.start()
 
     own_patches.wait()
@@ -149,29 +170,47 @@
     )
 
     own_tokens.wait()
-    for copy in z_copies:
-        copy.wait_recv()
-    zflat[...] = zbuf[...].astype(f32).reshape(zflat.shape)
-    for t in range(part):
-        gbuf[y * part + t, x] = zflat[pl.ds(t, NZ, stride=part), :].astype(bf16)
-
-    g_copies = {}
     mine = gbuf.at[pl.ds(y * part, part), x]
-    for n, (dx, dy) in enumerate(xy_steps):
-        copy = remote(
-            mine, mine, g_send.at[n], g_recv.at[n],
-            device(along(x, dx, NX), along(y, dy, NY), z, core),
+
+    def g_copy(source_core, dx, dy):
+        n = dy * NX + dx
+        return remote(
+            mine if source_core == 0 else stage, mine,
+            g_send.at[source_core, n], g_recv.at[n],
+            device(along(x, dx, NX), along(y, dy, NY), z, source_core),
         )
-        copy.start()
-        g_copies[dx, dy] = copy
+
+    @pl.when(core == 0)
+    def _():
+        for d in z_steps:
+            z_copy(0, d).wait_recv()
+        zflat[...] = zbuf[0].astype(f32).reshape(zflat.shape)
+        for t in range(part):
+            gbuf[y * part + t, x] = zflat[pl.ds(t, NZ, stride=part), :].astype(bf16)
+        for dx, dy in xy_steps:
+            g_copy(0, dx, dy).start()
+        for d in z_steps:
+            z_copy(1, d).wait_recv()
+        zflat[...] = zbuf[1].astype(f32).reshape(zflat.shape)
+        for t in range(part):
+            stage[t] = zflat[pl.ds(t, NZ, stride=part), :].astype(bf16)
+        pl.semaphore_wait(ready, len(xy_steps))
+        for dx, dy in [(0, 0)] + xy_steps:
+            g_copy(1, dx, dy).start()
 
     ones = jnp.where(lax.broadcasted_iota(jnp.int32, (chunk, depth), 1) == 0, 1.0, 0.0).astype(bf16)
     rows_t = chunk // lanes_q
     l_copies = []
     for k, back in enumerate(y_steps):
         for dx in range(NX):
-            if (dx, back) in g_copies:
-                g_copies[dx, back].wait_recv()
+            if (dx, back) != (0, 0):
+                g_copy(0, dx, back).wait_recv()
+        if back == 0:
+
+            @pl.when(core == 1)
+            def _():
+                g_copy(0, 0, 0).wait_recv()
+
         gy = along(y, NY - back, NY)
 
         def scores(block):
@@ -351,7 +390,21 @@
     outs.append(pltpu.make_async_copy(qg_tile, qg_ref, local_sem.at[6]))
     outs[2].start()
 
-    for copy in z_copies + list(g_copies.values()) + l_copies + s_copies + x_copies:
+    for d in z_steps:
+        z_copy(core, d).wait_send()
+
+    @pl.when(core == 1)
+    def _():
+        z_copy(1, 0).wait_send()
+
+    @pl.when(core == 0)
+    def _():
+        for dx, dy in xy_steps:
+            g_copy(0, dx, dy).wait_send()
+        for dx, dy in [(0, 0)] + xy_steps:
+            g_copy(1, dx, dy).wait_send()
+
+    for copy in l_copies + s_copies + x_copies:
         copy.wait_send()
     for copy in [swap_patches, swap_counts, swap_loss, swap_grads]:
         copy.wait_send()
@@ -402,8 +455,9 @@
             vmem((1, 2 * lanes_q), f32),
             vmem((1, part, depth), f32),
             vmem((2, slab, depth), f32),
-            vmem((NZ, part, depth), bf16),
+            vmem((2, NZ, part, depth), bf16),
             vmem((NZ * part, depth), f32),
+            vmem((part, NZ, depth), bf16),
             vmem((query_len, NX, NZ, depth), bf16),
             vmem((4, slab, depth), bf16),
             vmem((4, slab, depth), bf16),
@@ -428,10 +482,11 @@
             vmem((NZ, part, depth), f32),
             vmem((2, slab, depth), f32),
             vmem((2, slab, depth), f32),
+            pltpu.SemaphoreType.REGULAR,
             dma((7,)),
             dma((4,)), dma((4,)),
-            dma((NZ,)), dma((NZ,)),
-            dma((peers,)), dma((peers,)),
+            dma((NZ,)), dma((2, NZ)),
+            dma((2, peers + 1)), dma((peers + 1,)),
             dma((NY, NY - 1)), dma((NY, NY - 1)),
             dma((NZ,)), dma((NZ,)),
             dma((NX,)), dma((NX,)),

time: 65.9 us -> 68.3 us (1.036)
  Pallas kernels: 64.8 us -> 67.2 us
    pallas_call x1, Pallas kernels: 63 us -> 65.4 us  [shards(): pl.pallas_call(functools.partial(kernel, sizes), out_shape=shapes[::-1],...]
where the time goes in v3:
time: 68.3 us; the launch traced here: 67.8 us
  Pallas kernels  67.2 us (98%)
    pallas_call x1, Pallas kernels, shards(): pl.pallas_call(functools.partial(kernel, sizes), out_shape=shapes[::-1],...  65.4 us
    pallas_call x1, Pallas kernels, shards(): pl.pallas_call(hand_on, out_shape=shapes, in_specs=[hbm] * 3, out_specs=[...  1.77 us

profile of v3, /device:TPU:6, one launch (start us, length us, event | category | flops | bytes accessed | tf_op | source)
XLA Modules:
  0.0 67.8 jit_solution(16303168676757618432)
XLA Ops:
  0.6 65.4 %shard_map.67 = (f32[1,128]{1,0:T(1,128)}, f32[1,8,128]{2,1,0:T(8,128)}, f32[2,384,128]{2,1,0:T(8,128)}) custom-call(bf16[1,32,128]{2,1,0:T(8,128)(2,1)} %tok_ref.1, bf16[2,384,128]{2,1,0:T(8,128)(2,1)} %pat_ref.1, s32[2]{0:T(128)} %cnt_ref.1, s32[1,128]{1,0:T(1,128)} %bitcast.2), custom_call_target="tpu_custom_call" | custom-call | tf_op jit(solution)/shard_map/pallas_call | solution.py:447
  66.0 1.8 %shard_map.68 = (f32[2,384,128]{2,1,0:T(8,128)}, f32[1,8,128]{2,1,0:T(8,128)}, f32[1,128]{1,0:T(1,128)}) custom-call(f32[2,384,128]{2,1,0:T(8,128)} %get-tuple-element.9.refs_0_, f32[1,8,128]{2,1,0:T(8,128)} %get-tuple-element.10.refs_1_, f32[1,128]{1,0:T(1,128)} %get-tuple-element.11.refs_2_), custom_call_target="tpu_custom_call" | custom-call | tf_op jit(solution)/shard_map/pallas_call | solution.py:500

commit v4 on v3

--- a/solution.py
+++ b/solution.py
@@ -172,13 +172,13 @@
     own_tokens.wait()
     mine = gbuf.at[pl.ds(y * part, part), x]
 
-    def g_copy(source_core, dx, dy):
-        n = dy * NX + dx
+    def g_copy(dx, dy):
         return remote(
-            mine if source_core == 0 else stage, mine,
-            g_send.at[source_core, n], g_recv.at[n],
-            device(along(x, dx, NX), along(y, dy, NY), z, source_core),
+            mine, mine, g_send.at[dy * NX + dx], g_recv.at[dy * NX + dx],
+            device(along(x, dx, NX), along(y, dy, NY), z, core),
         )
+
+    hand_tokens = remote(stage, mine, g_send.at[0], g_recv.at[0], partner)
 
     @pl.when(core == 0)
     def _():
@@ -188,15 +188,20 @@
         for t in range(part):
             gbuf[y * part + t, x] = zflat[pl.ds(t, NZ, stride=part), :].astype(bf16)
         for dx, dy in xy_steps:
-            g_copy(0, dx, dy).start()
+            g_copy(dx, dy).start()
         for d in z_steps:
             z_copy(1, d).wait_recv()
         zflat[...] = zbuf[1].astype(f32).reshape(zflat.shape)
         for t in range(part):
             stage[t] = zflat[pl.ds(t, NZ, stride=part), :].astype(bf16)
         pl.semaphore_wait(ready, len(xy_steps))
-        for dx, dy in [(0, 0)] + xy_steps:
-            g_copy(1, dx, dy).start()
+        hand_tokens.start()
+
+    @pl.when(core == 1)
+    def _():
+        hand_tokens.wait_recv()
+        for dx, dy in xy_steps:
+            g_copy(dx, dy).start()
 
     ones = jnp.where(lax.broadcasted_iota(jnp.int32, (chunk, depth), 1) == 0, 1.0, 0.0).astype(bf16)
     rows_t = chunk // lanes_q
@@ -204,13 +209,7 @@
     for k, back in enumerate(y_steps):
         for dx in range(NX):
             if (dx, back) != (0, 0):
-                g_copy(0, dx, back).wait_recv()
-        if back == 0:
-
-            @pl.when(core == 1)
-            def _():
-                g_copy(0, 0, 0).wait_recv()
-
+                g_copy(dx, back).wait_recv()
         gy = along(y, NY - back, NY)
 
         def scores(block):
@@ -399,11 +398,10 @@
 
     @pl.when(core == 0)
     def _():
-        for dx, dy in xy_steps:
-            g_copy(0, dx, dy).wait_send()
-        for dx, dy in [(0, 0)] + xy_steps:
-            g_copy(1, dx, dy).wait_send()
-
+        hand_tokens.wait_send()
+
+    for dx, dy in xy_steps:
+        g_copy(dx, dy).wait_send()
     for copy in l_copies + s_copies + x_copies:
         copy.wait_send()
     for copy in [swap_patches, swap_counts, swap_loss, swap_grads]:
@@ -416,8 +414,13 @@
 
 def hand_on(*refs):
     sources, targets, tiles, sem = refs[:3], refs[3:6], refs[6:9], refs[9]
-    takes = [pltpu.make_async_copy(s, t, sem.at[i]) for i, (s, t) in enumerate(zip(sources, tiles))]
-    gives = [pltpu.make_async_copy(t, o, sem.at[i]) for i, (t, o) in enumerate(zip(tiles, targets))]
+    rows = sources[0].shape[1] // 2
+    parts = [(0, (i, pl.ds(j * rows, rows))) for i in range(2) for j in range(2)] + [(1, ()), (2, ())]
+    takes, gives = [], []
+    for n, (i, where) in enumerate(parts):
+        source, tile, target = (r[i].at[where] if where else r[i] for r in (sources, tiles, targets))
+        takes.append(pltpu.make_async_copy(source, tile, sem.at[0, n]))
+        gives.append(pltpu.make_async_copy(tile, target, sem.at[1, n]))
     for copy in takes:
         copy.start()
     for take, give in zip(takes, gives):
@@ -486,7 +489,7 @@
             dma((7,)),
             dma((4,)), dma((4,)),
             dma((NZ,)), dma((2, NZ)),
-            dma((2, peers + 1)), dma((peers + 1,)),
+            dma((peers + 1,)), dma((peers + 1,)),
             dma((NY, NY - 1)), dma((NY, NY - 1)),
             dma((NZ,)), dma((NZ,)),
             dma((NX,)), dma((NX,)),
@@ -502,7 +505,7 @@
         out_shape=shapes,
         in_specs=[hbm] * 3,
         out_specs=[hbm] * 3,
-        scratch_shapes=[vmem(shape.shape, f32) for shape in shapes] + [dma((3,))],
+        scratch_shapes=[vmem(shape.shape, f32) for shape in shapes] + [dma((2, 6))],
     )(page_grad, query_grad, loss)
     return (loss.reshape(2 * lanes_q), query_grad, page_grad)
 

time: 68.3 us -> 67.1 us (0.982)
  Pallas kernels: 67.2 us -> 66.2 us
    pallas_call x1, Pallas kernels: 65.4 us -> 64.4 us  [shards(): pl.pallas_call(functools.partial(kernel, sizes), out_shape=shapes[::-1],...]
where the time goes in v4:
time: 67.1 us; the launch traced here: 66.9 us
  Pallas kernels  66.2 us (99%)
    pallas_call x1, Pallas kernels, shards(): pl.pallas_call(functools.partial(kernel, sizes), out_shape=shapes[::-1],...  64.4 us
    pallas_call x1, Pallas kernels, shards(): pl.pallas_call(hand_on, out_shape=shapes, in_specs=[hbm] * 3, out_specs=[...  1.78 us

profile of v4, /device:TPU:6, one launch (start us, length us, event | category | flops | bytes accessed | tf_op | source)
XLA Modules:
  0.0 66.9 jit_solution(1173787489357116309)
XLA Ops:
  0.6 64.4 %shard_map.67 = (f32[1,128]{1,0:T(1,128)}, f32[1,8,128]{2,1,0:T(8,128)}, f32[2,384,128]{2,1,0:T(8,128)}) custom-call(bf16[1,32,128]{2,1,0:T(8,128)(2,1)} %tok_ref.1, bf16[2,384,128]{2,1,0:T(8,128)(2,1)} %pat_ref.1, s32[2]{0:T(128)} %cnt_ref.1, s32[1,128]{1,0:T(1,128)} %bitcast.2), custom_call_target="tpu_custom_call" | custom-call | tf_op jit(solution)/shard_map/pallas_call | solution.py:450
  65.1 1.8 %shard_map.68 = (f32[2,384,128]{2,1,0:T(8,128)}, f32[1,8,128]{2,1,0:T(8,128)}, f32[1,128]{1,0:T(1,128)}) custom-call(f32[2,384,128]{2,1,0:T(8,128)} %get-tuple-element.9.refs_0_, f32[1,8,128]{2,1,0:T(8,128)} %get-tuple-element.10.refs_1_, f32[1,128]{1,0:T(1,128)} %get-tuple-element.11.refs_2_), custom_call_target="tpu_custom_call" | custom-call | tf_op jit(solution)/shard_map/pallas_call | solution.py:503

commit v5 on v2

--- a/solution.py
+++ b/solution.py
@@ -41,11 +41,11 @@
 
 def kernel(
     sizes, tok_ref, pat_ref, cnt_ref, pos_ref, loss_ref, qg_ref, pg_ref,
-    counts, pos_row, loss_row, qg_tile, pg_tile,
+    counts, pos_row,
     zbuf, zflat, gbuf, pbuf, bias, ptran, cbuf, ebuf, coef, mbuf, lbuf, erbuf, rbuf,
-    held_a, held_b, softz, softx, lossbuf, sendbuf, ownbuf, recvbuf, zsum, zsend, zrecv, pgsend, pgrecv,
+    held_a, held_b, softs, lossbuf, sendbuf, ownbuf, recvbuf, zsum, zsend, zrecv, pgsend, pgrecv,
     local_sem, core_send, core_recv, z_send, z_recv, g_send, g_recv, l_send, l_recv,
-    s_send, s_recv, x_send, x_recv, r_send, r_recv, q_send, q_recv,
+    s_send, s_recv, r_send, r_recv, q_send, q_recv,
 ):
     NX, NY, NZ = sizes
     lanes_q = NX * NZ
@@ -155,23 +155,32 @@
     for t in range(part):
         gbuf[y * part + t, x] = zflat[pl.ds(t, NZ, stride=part), :].astype(bf16)
 
+    pieces = group // chunk
+    rows_t = chunk // lanes_q
     g_copies = {}
-    mine = gbuf.at[pl.ds(y * part, part), x]
-    for n, (dx, dy) in enumerate(xy_steps):
-        copy = remote(
-            mine, mine, g_send.at[n], g_recv.at[n],
-            device(along(x, dx, NX), along(y, dy, NY), z, core),
-        )
+    for dx, dy in xy_steps:
+        count = pieces if dy == y_steps[-1] else 1
+        for h in range(count):
+            n = (h * NY + dy) * NX + dx
+            mine = gbuf.at[pl.ds(y * part + h * (part // count), part // count), x]
+            g_copies[dx, dy, h] = remote(
+                mine, mine, g_send.at[n], g_recv.at[n],
+                device(along(x, dx, NX), along(y, dy, NY), z, core),
+            )
+    for (dx, dy, h), copy in sorted(
+        g_copies.items(), key=lambda item: (y_steps.index(item[0][1]), item[0][2])
+    ):
         copy.start()
-        g_copies[dx, dy] = copy
 
     ones = jnp.where(lax.broadcasted_iota(jnp.int32, (chunk, depth), 1) == 0, 1.0, 0.0).astype(bf16)
-    rows_t = chunk // lanes_q
     l_copies = []
     for k, back in enumerate(y_steps):
-        for dx in range(NX):
-            if (dx, back) in g_copies:
-                g_copies[dx, back].wait_recv()
+        def arrive(h):
+            for dx in range(NX):
+                if (dx, back, h) in g_copies:
+                    g_copies[dx, back, h].wait_recv()
+
+        arrive(0)
         gy = along(y, NY - back, NY)
 
         def scores(block):
@@ -197,8 +206,14 @@
         blocks = 4 * (group // chunk)
         top = scores(0)
         for block in range(blocks):
-            following = scores(block + 1) if block + 1 < blocks else None
-            exponents(block, top)
+            after = block + 1
+            late = after < blocks and after % 4 == 0 and back == y_steps[-1]
+            if late:
+                exponents(block, top)
+                arrive(after // 4)
+            following = scores(after) if after < blocks else None
+            if not late:
+                exponents(block, top)
             top = following
         for n, dy in enumerate(y_steps[1:]):
             copy = remote(
@@ -221,32 +236,30 @@
     page_id = (chip * 4 + lax.broadcasted_iota(jnp.int32, (4, wide), 0)).astype(f32)
     is_positive = page_id == positive
 
-    softz[z, 0:1, :] = merge_lse(logits[:, None, :], 1.0)
-    softz[z, 1:2, :] = jnp.sum(jnp.where(is_positive, logits, 0.0), axis=0, keepdims=True)
+    low = lax.broadcasted_iota(jnp.int32, (1, wide), 1) < lanes_q
+    here = x * NZ + z
+    softs[here] = jnp.where(
+        low, merge_lse(logits[:, None, :], 1.0),
+        jnp.sum(jnp.where(is_positive, logits, 0.0), axis=0, keepdims=True),
+    )
     s_copies = []
-    for d in reversed(z_steps):
-        copy = remote(
-            softz.at[z], softz.at[z], s_send.at[d], s_recv.at[d],
-            device(x, y, along(z, d, NZ), core),
-        )
-        copy.start()
-        s_copies.append(copy)
+    for d in reversed(ring_offsets(NZ)):
+        for dx in reversed(ring_offsets(NX)):
+            if (dx, d) == (0, 0):
+                continue
+            copy = remote(
+                softs.at[here], softs.at[here], s_send.at[dx, d], s_recv.at[dx, d],
+                device(along(x, dx, NX), y, along(z, d, NZ), core),
+            )
+            copy.start()
+            s_copies.append(copy)
     for copy in s_copies:
         copy.wait_recv()
-    softx[x, 0:1, :] = merge_lse(softz[:, 0:1, :], 1.0)
-    softx[x, 1:2, :] = jnp.sum(softz[:, 1:2, :], axis=0)
-    x_copies = []
-    for d in ring_offsets(NX)[1:]:
-        copy = remote(
-            softx.at[x], softx.at[x], x_send.at[d], x_recv.at[d],
-            device(along(x, d, NX), y, z, core),
-        )
-        copy.start()
-        x_copies.append(copy)
-    for copy in x_copies:
-        copy.wait_recv()
-    all_lse = merge_lse(softx[:, 0:1, :], 1.0)
-    lossbuf[core] = all_lse - jnp.sum(softx[:, 1:2, :], axis=0)
+    everyone = softs[...]
+    all_lse = merge_lse(everyone, 1.0)
+    all_lse = jnp.where(low, all_lse, pltpu.roll(all_lse, lanes_q, 1))
+    all_pos = jnp.sum(everyone, axis=0)
+    lossbuf[core] = all_lse - pltpu.roll(all_pos, lanes_q, 1)
     swap_loss = remote(lossbuf.at[core], lossbuf.at[core], core_send.at[2], core_recv.at[2], partner)
     swap_loss.start()
     weights = (jnp.exp(logits - all_lse) - is_positive.astype(f32)) / page_temp
@@ -258,14 +271,16 @@
     for back in reversed(y_steps):
         gy = along(y, NY - back, NY)
 
-        def backward(p, carry):
-            coef[gy, p] = (ebuf[gy, p] * rbuf[gy, pl.ds(p, 1), :]).astype(bf16)
-            return carry
-
-        lax.fori_loop(0, 4, backward, 0)
-
-        def grads(piece, carry):
-            lanes = pl.ds(pl.multiple_of(piece * chunk, chunk), chunk)
+        for piece in range(pieces):
+            lanes = slice(piece * chunk, (piece + 1) * chunk)
+
+            def backward(p, carry):
+                coef[gy, p, :, lanes] = (
+                    ebuf[gy, p, :, lanes] * rbuf[gy, pl.ds(p, 1), lanes]
+                ).astype(bf16)
+                return carry
+
+            lax.fori_loop(0, 4, backward, 0)
             across = jnp.dot(
                 ptran[...], coef[gy, :, :, lanes].reshape(4 * slab, chunk),
                 preferred_element_type=f32,
@@ -274,21 +289,19 @@
             sendbuf[pl.ds(gy * part + piece * rows_t, rows_t)] = rows.astype(bf16)
             if back == 0:
                 ownbuf[pl.ds(piece * rows_t, rows_t)] = rows
-            return carry
-
-        lax.fori_loop(0, group // chunk, grads, 0)
-        for dx in range(NX):
             dy = (NY - back) % NY
-            if (dx, dy) == (0, 0):
-                continue
-            n = xy_steps.index((dx, dy))
-            xx = along(x, dx, NX)
-            copy = remote(
-                sendbuf.at[pl.ds(gy * part, part), xx], recvbuf.at[x * NY + y],
-                r_send.at[n], r_recv.at[n], device(xx, gy, z, core),
-            )
-            copy.start()
-            r_copies.append((copy, dx, dy))
+            for dx in reversed(ring_offsets(NX)):
+                if (dx, dy) == (0, 0):
+                    continue
+                n = (piece * NY + dy) * NX + dx
+                xx = along(x, dx, NX)
+                copy = remote(
+                    sendbuf.at[pl.ds(gy * part + piece * rows_t, rows_t), xx],
+                    recvbuf.at[x * NY + y, pl.ds(piece * rows_t, rows_t)],
+                    r_send.at[n], r_recv.at[n], device(xx, gy, z, core),
+                )
+                copy.start()
+                r_copies.append((copy, dx, dy, piece))
 
     def page_part(p):
         total = jnp.zeros((slab, depth), f32)
@@ -306,8 +319,10 @@
     swap_grads.start()
 
     total = ownbuf[:, pl.ds(x, 1)].reshape(part * NZ, depth)
-    for copy, dx, dy in r_copies:
+    for copy, dx, dy, piece in sorted(r_copies, key=lambda item: item[3]):
         copy.wait_recv()
+        if piece + 1 < pieces:
+            continue
         source = along(x, NX - dx, NX) * NY + along(y, NY - dy, NY)
         total = total + recvbuf[source].astype(f32).reshape(part * NZ, depth)
     zsum[...] = total
@@ -323,14 +338,12 @@
         q_copies.append((copy, d))
 
     def own_page(i, carry):
-        pg_tile[i] = page_part(2 * core + i)
+        pg_ref[i] = page_part(2 * core + i)
         return carry
 
     lax.fori_loop(0, 2, own_page, 0)
     swap_grads.wait_recv()
-    pg_tile[...] += pgrecv[...]
-    outs = [pltpu.make_async_copy(pg_tile, pg_ref, local_sem.at[4])]
-    outs[0].start()
+    pg_ref[...] += pgrecv[...]
 
     swap_loss.wait_recv()
     row = lax.broadcasted_iota(jnp.int32, (wide, 2 * lanes_q), 0)
@@ -339,38 +352,28 @@
     for c in range(2):
         spread = jnp.logical_and(col == 2 * row + c, row < lanes_q).astype(f32).astype(bf16)
         loss = loss + onehot_dot(lossbuf[c], spread)
-    loss_row[...] = loss
-    outs.append(pltpu.make_async_copy(loss_row, loss_ref, local_sem.at[5]))
-    outs[1].start()
+    loss_ref[...] = loss
 
     total = zsend[z]
     for copy, d in q_copies:
         copy.wait_recv()
         total = total + zrecv[along(z, NZ - d, NZ)]
-    qg_tile[0] = total
-    outs.append(pltpu.make_async_copy(qg_tile, qg_ref, local_sem.at[6]))
-    outs[2].start()
-
-    for copy in z_copies + list(g_copies.values()) + l_copies + s_copies + x_copies:
+    qg_ref[0] = total
+
+    for copy in z_copies + list(g_copies.values()) + l_copies + s_copies:
         copy.wait_send()
     for copy in [swap_patches, swap_counts, swap_loss, swap_grads]:
         copy.wait_send()
     for copy, *_ in r_copies + q_copies:
         copy.wait_send()
-    for copy in outs:
-        copy.wait()
 
 
 def hand_on(*refs):
-    sources, targets, tiles, sem = refs[:3], refs[3:6], refs[6:9], refs[9]
-    takes = [pltpu.make_async_copy(s, t, sem.at[i]) for i, (s, t) in enumerate(zip(sources, tiles))]
-    gives = [pltpu.make_async_copy(t, o, sem.at[i]) for i, (t, o) in enumerate(zip(tiles, targets))]
-    for copy in takes:
+    sources, targets, sem = refs[:3], refs[3:6], refs[6]
+    copies = [pltpu.make_async_copy(s, t, sem.at[i]) for i, (s, t) in enumerate(zip(sources, targets))]
+    for copy in copies:
         copy.start()
-    for take, give in zip(takes, gives):
-        take.wait()
-        give.start()
-    for copy in gives:
+    for copy in copies:
         copy.wait()
 
 
@@ -382,7 +385,7 @@
     lanes_q = NX * NZ
     group = part * lanes_q
     wide = 2 * lanes_q
-    peers = NX * NY - 1
+    pieces = group // min(lane_chunk, group)
     vmem = pltpu.VMEM
     dma = pltpu.SemaphoreType.DMA
     shapes = [
@@ -393,15 +396,12 @@
     hbm = pl.BlockSpec(memory_space=pltpu.HBM)
     loss, query_grad, page_grad = pl.pallas_call(
         functools.partial(kernel, sizes),
-        out_shape=shapes[::-1],
+        out_shape=[vmem(shape.shape, f32) for shape in shapes[::-1]],
         in_specs=[hbm] * 4,
-        out_specs=[hbm] * 3,
+        out_specs=[pl.BlockSpec(memory_space=pltpu.VMEM)] * 3,
         scratch_shapes=[
             pltpu.SMEM((2,), jnp.int32),
             vmem((1, 2 * lanes_q), jnp.int32),
-            vmem((1, 2 * lanes_q), f32),
-            vmem((1, part, depth), f32),
-            vmem((2, slab, depth), f32),
             vmem((NZ, part, depth), bf16),
             vmem((NZ * part, depth), f32),
             vmem((query_len, NX, NZ, depth), bf16),
@@ -417,8 +417,7 @@
             vmem((NY, 4, group), f32),
             vmem((slab, min(lane_chunk, group)), f32),
             vmem((slab, min(lane_chunk, group)), f32),
-            vmem((NZ, 2, wide), f32),
-            vmem((NX, 2, wide), f32),
+            vmem((NX * NZ, 1, wide), f32),
             vmem((2, 1, wide), f32),
             vmem((query_len, NX, NZ, depth), bf16),
             vmem((part, NX, NZ, depth), f32),
@@ -428,14 +427,13 @@
             vmem((NZ, part, depth), f32),
             vmem((2, slab, depth), f32),
             vmem((2, slab, depth), f32),
-            dma((7,)),
+            dma((4,)),
             dma((4,)), dma((4,)),
             dma((NZ,)), dma((NZ,)),
-            dma((peers,)), dma((peers,)),
+            dma((pieces * NX * NY,)), dma((pieces * NX * NY,)),
             dma((NY, NY - 1)), dma((NY, NY - 1)),
-            dma((NZ,)), dma((NZ,)),
-            dma((NX,)), dma((NX,)),
-            dma((peers,)), dma((peers,)),
+            dma((NX, NZ)), dma((NX, NZ)),
+            dma((pieces * NX * NY,)), dma((pieces * NX * NY,)),
             dma((NZ,)), dma((NZ,)),
         ],
         compiler_params=pltpu.CompilerParams(
@@ -445,10 +443,10 @@
     page_grad, query_grad, loss = pl.pallas_call(
         hand_on,
         out_shape=shapes,
-        in_specs=[hbm] * 3,
+        in_specs=[pl.BlockSpec(memory_space=pltpu.VMEM)] * 3,
         out_specs=[hbm] * 3,
-        scratch_shapes=[vmem(shape.shape, f32) for shape in shapes] + [dma((3,))],
-    )(page_grad, query_grad, loss)
+        scratch_shapes=[dma((3,))],
+    )(*(pltpu.with_memory_space_constraint(a, pltpu.VMEM) for a in (page_grad, query_grad, loss)))
     return (loss.reshape(2 * lanes_q), query_grad, page_grad)
 
 

time: 65.9 us -> 64.4 us (0.977)
  Pallas kernels: 64.8 us -> 62.7 us
    pallas_call x2, Pallas kernels: 64.8 us -> 62.7 us  [the longest x1 61.9 us: shards(): pl.pallas_call(functools.partial(kernel, sizes), out_shape=[vmem(shape.sh...]
where the time goes in v5:
time: 64.4 us; the launch traced here: 63.3 us
  Pallas kernels  62.7 us (97%)
    pallas_call x1, Pallas kernels, shards(): pl.pallas_call(functools.partial(kernel, sizes), out_shape=[vmem(shape.sh...  61.9 us

profile of v5, /device:TPU:6, one launch (start us, length us, event | category | flops | bytes accessed | tf_op | source)
XLA Modules:
  0.0 63.3 jit_solution(1257819067019247913)
XLA Ops:
  0.6 61.9 %shard_map.67 = (f32[1,128]{1,0:T(1,128)S(1)}, f32[1,8,128]{2,1,0:T(8,128)S(1)}, f32[2,384,128]{2,1,0:T(8,128)S(1)}) custom-call(bf16[1,32,128]{2,1,0:T(8,128)(2,1)} %tok_ref.1, bf16[2,384,128]{2,1,0:T(8,128)(2,1)} %pat_ref.1, s32[2]{0:T(128)} %cnt_ref.1, s32[1,128]{1,0:T(1,128)} %bitcast.2), custom_call_target="tpu_custom_call" | custom-call | tf_op jit(solution)/shard_map/pallas_call | solution.py:397
  62.5 0.8 %shard_map.68 = (f32[2,384,128]{2,1,0:T(8,128)}, f32[1,8,128]{2,1,0:T(8,128)}, f32[1,128]{1,0:T(1,128)}) custom-call(f32[2,384,128]{2,1,0:T(8,128)S(1)} %get-tuple-element.9.refs_0_, f32[1,8,128]{2,1,0:T(8,128)S(1)} %get-tuple-element.10.refs_1_, f32[1,128]{1,0:T(1,128)S(1)} %get-tuple-element.11.refs_2_), custom_call_target="tpu_custom_call" | custom-call | tf_op jit(solution)/shard_map/pallas_call | solution.py:443

commit v6 on v5

--- a/solution.py
+++ b/solution.py
@@ -12,7 +12,7 @@
 page_temp = 0.02
 neg_large = -1e30
 chips_z = 16
-lane_chunk = 256
+lane_chunk = 512
 MESH = pl.DeviceIdType.MESH
 f32, bf16 = jnp.float32, jnp.bfloat16
 

time: 64.4 us -> 62.8 us (0.975); the launches traced: 63.3 us -> 62.7 us
  Pallas kernels: 62.7 us -> 62 us
where the time goes in v6:
time: 62.8 us; the launch traced here: 62.7 us
  Pallas kernels  62 us (99%)
  between operations  0.64 us (1%)
    pallas_call x1, Pallas kernels, shards(): pl.pallas_call(functools.partial(kernel, sizes), out_shape=[vmem(shape.sh...  61.2 us

profile of v6, /device:TPU:6, one launch (start us, length us, event | category | flops | bytes accessed | tf_op | source)
XLA Modules:
  0.0 62.7 jit_solution(14374412872055848763)
XLA Ops:
  0.6 61.2 %shard_map.67 = (f32[1,128]{1,0:T(1,128)S(1)}, f32[1,8,128]{2,1,0:T(8,128)S(1)}, f32[2,384,128]{2,1,0:T(8,128)S(1)}) custom-call(bf16[1,32,128]{2,1,0:T(8,128)(2,1)} %tok_ref.1, bf16[2,384,128]{2,1,0:T(8,128)(2,1)} %pat_ref.1, s32[2]{0:T(128)} %cnt_ref.1, s32[1,128]{1,0:T(1,128)} %bitcast.2), custom_call_target="tpu_custom_call" | custom-call | tf_op jit(solution)/shard_map/pallas_call | solution.py:397
  61.9 0.8 %shard_map.68 = (f32[2,384,128]{2,1,0:T(8,128)}, f32[1,8,128]{2,1,0:T(8,128)}, f32[1,128]{1,0:T(1,128)}) custom-call(f32[2,384,128]{2,1,0:T(8,128)S(1)} %get-tuple-element.9.refs_0_, f32[1,8,128]{2,1,0:T(8,128)S(1)} %get-tuple-element.10.refs_1_, f32[1,128]{1,0:T(1,128)S(1)} %get-tuple-element.11.refs_2_), custom_call_target="tpu_custom_call" | custom-call | tf_op jit(solution)/shard_map/pallas_call | solution.py:443
